TPU v7x, 256 devices: a whole 4x4x8 slice. The times are simulated.
256 devices in a mesh: blk: 64 (over y, z, core), pair: 4 (over x).
Axes of the slice: x: 4, y: 4, z: 8, core: 2. Of those that a mesh axis runs over, the one named last changes fastest.
Arguments:
- raw_strain: bfloat16 [4, 9216, 8192], P('pair', 'blk'), may hold values from -6 to 6
- aa_taps: bfloat16 [64], replicated, may hold values from -0.75 to 0.75
- white_taps: bfloat16 [255], replicated, may hold values from -0.375 to 0.375
- src_channels: int32 [64, 64], replicated, may hold values from 0 to 8191, as said below
- recv_lo: int32 [64, 64], P('blk'), may hold values from 0 to 63
- recv_hi: int32 [64, 64], P('blk'), may hold values from 65 to 128
Outputs:
- xcorr: float32 [64, 1024, 64, 128], P('blk', 'pair')
Inputs may be any that keep to these rules, and one draw needn't show every extreme that they name: `src_channels`: row b lists 64 distinct channels: exactly 2 channels from each of 32 distinct tiles and none from the other tiles; tile of channel c is c // 128.
All inputs are finite; a program needn't handle non-finite values.
Results may differ from a plain program's by a relative error of at most 0.0052.
Values may be sent and summed in bfloat16 or wider, within the bound.
A program may use at most 128 MiB of HBM per device.

v0:
```python
import math

import jax
import jax.numpy as jnp
from jax import lax
from jax.sharding import PartitionSpec as P

DECIM = 8
KA = 64
LAGS = 1024
CAP = 2


def extended_2(cells, sides, width):
    for axis, dim in sides:
        count = lax.axis_size(axis)
        ends = count - 1
        head = lax.slice_in_dim(cells, 0, width, axis=dim)
        tail = lax.slice_in_dim(cells, cells.shape[dim] - width, cells.shape[dim], axis=dim)
        cells = jnp.concatenate(
            [
                lax.ppermute(tail, axis, [(i, (i + 1) % count) for i in range(ends)]),
                cells,
                lax.ppermute(head, axis, [((i + 1) % count, i) for i in range(ends)]),
            ],
            axis=dim,
        )
    return cells


def whiten_matrix(white_taps, length):
    n_taps = white_taps.shape[0]
    half = n_taps // 2
    left = length - 1 - half
    right = 2 * length - 1 - left - n_taps
    spread = jnp.pad(white_taps, (left, right))
    rolled = jnp.roll(spread, length)
    tiled = jnp.tile(rolled, length)[: length * (2 * length - 2)]
    return tiled.reshape(length, 2 * length - 2)[:, :length]


def body(raw_strain, aa_taps, white_taps, src_channels, recv_lo, recv_hi):
    raw_len = raw_strain.shape[1]
    short_len = raw_len // DECIM
    channels = raw_strain.shape[2]
    n_blocks = lax.axis_size("blk")
    tile = channels // n_blocks
    seg_len = short_len * n_blocks
    span = seg_len - LAGS
    extended = extended_2(raw_strain[0], (("blk", 0),), KA // 2)
    out_rows = jnp.arange(short_len)[:, None]
    in_cols = jnp.arange(raw_len + KA)[None, :]
    offset = in_cols - DECIM * out_rows
    valid = (offset >= 0) & (offset < KA)
    aa_matrix = jnp.where(valid, aa_taps[jnp.clip(offset, 0, KA - 1)], jnp.zeros((), aa_taps.dtype))
    decimated = jnp.dot(aa_matrix, extended, preferred_element_type=jnp.float32).astype(
        jnp.bfloat16
    )
    white_matrix = whiten_matrix(white_taps, seg_len)
    n_src = src_channels.shape[1]
    n_tiles = src_channels.shape[0]
    tile_raw = lax.all_to_all(decimated, "blk", split_axis=1, concat_axis=0, tiled=True)
    white_tile = jnp.dot(white_matrix, tile_raw, preferred_element_type=jnp.float32).astype(
        jnp.bfloat16
    )
    tile_of = src_channels // tile
    chan_of = src_channels - tile_of * tile
    same = tile_of[:, :, None] == tile_of[:, None, :]
    earlier = jnp.arange(n_src)[None, :] < jnp.arange(n_src)[:, None]
    slot_of = jnp.sum((same & earlier[None]).astype(jnp.int32), axis=2)
    mine = lax.axis_index("blk")
    belongs = tile_of == mine
    one_slot = (slot_of[:, :, None] == jnp.arange(CAP)[None, None, :]) & belongs[:, :, None]
    one_chan = chan_of[:, :, None] == jnp.arange(tile)[None, None, :]
    picker = jnp.einsum(
        "dkc,dkr->dcr",
        one_slot.astype(jnp.bfloat16),
        one_chan.astype(jnp.bfloat16),
        preferred_element_type=jnp.float32,
    ).astype(jnp.bfloat16)
    outgoing = jnp.einsum(
        "dcr,tr->dct", picker, white_tile, preferred_element_type=jnp.float32
    ).astype(jnp.bfloat16)
    incoming = lax.all_to_all(outgoing, "blk", split_axis=0, concat_axis=0, tiled=True)
    own_tiles = lax.dynamic_index_in_dim(tile_of, mine, 0, keepdims=False)
    own_slots = lax.dynamic_index_in_dim(slot_of, mine, 0, keepdims=False)
    selector = (own_tiles[:, None, None] == jnp.arange(n_tiles)[None, :, None]) & (
        own_slots[:, None, None] == jnp.arange(CAP)[None, None, :]
    )
    sources = jnp.einsum(
        "kec,ect->tk", selector.astype(jnp.bfloat16), incoming, preferred_element_type=jnp.float32
    ).astype(jnp.bfloat16)
    source_window = sources[LAGS // 2 : LAGS // 2 + span]
    lag_share = LAGS // lax.axis_size("pair")
    lag_start = lax.axis_index("pair") * lag_share
    lag_block = math.gcd(128, lag_share)
    n_lag_blocks = lag_share // lag_block
    initial = jnp.zeros((lag_share, n_src, tile), jnp.float32)
    total = initial
    tiles_in = lax.all_gather(white_tile[None], "pair", axis=0, tiled=True)
    sources_in = lax.all_gather(source_window[None], "pair", axis=0, tiled=True)
    for segment in range(tiles_in.shape[0]):
        window = lax.dynamic_slice_in_dim(tiles_in[segment], lag_start, span + lag_share, 0)
        parts = []
        for block in range(n_lag_blocks):
            base = block * lag_block
            hankel = jnp.stack(
                [window[base + shift : base + shift + span] for shift in range(lag_block)], 1
            )
            parts.append(
                jnp.einsum(
                    "tk,tjr->jkr", sources_in[segment], hankel, preferred_element_type=jnp.float32
                )
            )
        total = total + jnp.concatenate(parts, 0)
    scale = 1.0 / math.sqrt(span * lax.axis_size("pair"))
    position = jnp.arange(tile)[None, :]
    inside = (position >= recv_lo[0][:, None]) & (position < recv_hi[0][:, None])
    mask = jnp.where(inside, jnp.float32(scale), jnp.float32(0.0))
    return (total * mask[None])[None]


def solution(mesh):
    placed = (P("pair", "blk", None), P(), P(), P(), P("blk", None), P("blk", None))
    return jax.shard_map(
        body, mesh=mesh, in_specs=placed, out_specs=P("blk", "pair", None, None), check_vma=False
    )
```

profile of v0, /device:TPU:1, one launch (start us, length us, event | category | flops | bytes accessed | tf_op | source)
XLA Modules:
  0.0 202.3 jit_solution(10262311969563306636)
XLA Ops:
  6.5 0.0 copy-start
  6.5 1.3 slice_bitcast_fusion.1
  7.8 4.9 %collective-permute-start = (bf16[32,8192]{1,0:T(8,128)(2,1)S(1)}, bf16[32,8192]{1,0:T(8,128)(2,1)S(1)}, u32[]{:S(2)}, u32[]{:S(2)}) collective-permute-start(bf16[32,8192]{1,0:T(8,128)(2,1)S(1)} %get-tuple-element.5), channel_id=1, source_target_pairs={{0,4},{4,8},{8,12},{12,16},{16,20},{20,24},{24,28},{28,32},{32,36}... | collective-permute-start | bytes 1572872 | tf_op jit(solution)/shard_map/ppermute | solution.py:22
  12.8 1.9 collective-permute-start.1
  14.7 0.1 compare_select_fusion
  14.8 0.1 reshape.2337
  14.9 0.0 copy-done
  14.9 21.4 %gather_fusion = bf16[3744]{0:T(1024)(128)(2,1)S(1)} fusion(bf16[64]{0:T(256)(128)(2,1)S(1)} %copy-done, s32[4096]{0:T(1024)S(1)} %pad_clamp_fusion), kind=kCustom, calls=%fused_computation | custom fusion | bytes 29952 | tf_op jit(solution)/shard_map/gather | solution.py:55
  36.3 0.1 reshape.2336
  36.4 0.0 collective-permute-done
  36.4 0.0 collective-permute-done.1
  36.4 0.0 copy-start.3
  36.4 2.3 %convolution_convert_fusion = bf16[18,8192]{1,0:T(8,128)(2,1)S(1)} fusion(bf16[32,8192]{1,0:T(8,128)(2,1)S(1)} %collective-permute-done.1, bf16[144,8192]{1,0:T(8,128)(2,1)} %bitcast.4185, bf16[32,8192]{1,0:T(8,128)(2,1)S(1)} %collective-permute-done, bf16[18,208]{1,0:T(8,128)(2,1)S(1)} %reshape.2336, s32[18]{0:T(128)S(1)} %iota_multiply_fusion), kind=kOutput, calls=%fused_computation.1 | convolution fusion | flops 71731488 | bytes 3710344 | tf_op jit(solution)/shard_map/dot_general | solution.py:56
  38.7 0.1 copy.16
  38.8 1.0 copy.12
  39.8 13.1 %all-to-all-start = ((bf16[18,64,128]{2,0,1:T(8,128)(2,1)}), bf16[18,64,128]{2,0,1:T(8,128)(2,1)S(1)}, u32[]{:S(2)}, u32[]{:S(2)}) async-start(bf16[18,64,128]{2,0,1:T(8,128)(2,1)} %copy.12), calls=%async_computation | async-start | bytes 786432 | tf_op jit(solution)/shard_map/all_to_all | solution.py:62
  52.8 0.6 all-gather.4.cloned.1.call-start
  53.4 0.0 copy-done.3
  53.4 0.1 pad_slice_fusion.1
  53.5 2.7 %tile.4 = bf16[1152,2303]{1,0:T(8,128)(2,1)} broadcast(bf16[2303]{0:T(1024)(128)(2,1)S(1)} %pad_maximum_fusion), dimensions={1} | broadcast | bytes 5310718 | tf_op jit(solution)/shard_map/tile | solution.py:38
  56.2 14.8 %tile.10 = bf16[2653056]{0:T(1024)(128)(2,1)} reshape(bf16[1152,2303]{1,0:T(8,128)(2,1)} %tile.4) | data formatting | bytes 10612224 | tf_op jit(solution)/shard_map/tile | solution.py:38
  71.0 5.8 %slice.5204 = bf16[2651904]{0:T(1024)(128)(2,1)} slice(bf16[2653056]{0:T(1024)(128)(2,1)} %tile.10), slice={[0:2651904]} | slice | bytes 10607616 | tf_op jit(solution)/shard_map/slice | solution.py:38
  76.8 0.0 copy-start.2
  76.8 13.2 %reshape.2334 = bf16[1152,2302]{1,0:T(8,128)(2,1)} reshape(bf16[2651904]{0:T(1024)(128)(2,1)} %slice.5204) | data formatting | bytes 10607616 | tf_op jit(solution)/shard_map/reshape | solution.py:39
  90.0 0.0 copy-start.4
  90.0 0.0 copy-start.5
  90.0 0.0 copy-done.2
  90.1 0.0 all-to-all-done
  90.1 0.1 all_to_all.20
  90.2 3.3 %fusion.10 = bf16[1152,128]{1,0:T(8,128)(2,1)} fusion(bf16[1152,128]{1,0:T(8,128)(2,1)S(1)} %all_to_all.20, bf16[1152,2302]{1,0:T(8,128)(2,1)} %reshape.2334), kind=kOutput, calls=%fused_computation.13 | convolution fusion | flops 339886080 | bytes 3244032 | tf_op jit(solution)/shard_map/dot_general | solution.py:63
  93.5 0.0 all-gather.4.cloned.1.call-update
  93.5 1.9 convert_reduce_fusion
  95.5 0.9 fusion.14
  96.4 1.2 convolution_convert_fusion.1
  97.6 1.0 copy.14
  98.6 10.3 %all-to-all-start.1 = ((bf16[64,2,1152]{2,1,0:T(2,128)(2,1)}), bf16[64,2,1152]{2,1,0:T(2,128)(2,1)S(1)}, u32[]{:S(2)}, u32[]{:S(2)}) async-start(bf16[64,2,1152]{2,1,0:T(2,128)(2,1)} %copy.14), calls=%async_computation.1 | async-start | bytes 589824 | tf_op jit(solution)/shard_map/all_to_all | solution.py:84
  109.0 0.1 iota_compare_fusion.6
  109.0 0.0 copy-done.4
  109.0 0.0 copy-done.5
  109.1 0.1 fusion.26
  109.1 12.5 %all-to-all-done.1 = bf16[64,2,1152]{2,1,0:T(2,128)(2,1)S(1)} async-done(((bf16[64,2,1152]{2,1,0:T(2,128)(2,1)}), bf16[64,2,1152]{2,1,0:T(2,128)(2,1)S(1)}, u32[]{:S(2)}, u32[]{:S(2)}) %all-to-all-start.1) | async-done | bytes 294944 | tf_op jit(solution)/shard_map/all_to_all | solution.py:84
  121.6 0.3 convolution_bitcast_fusion
  121.9 9.0 %all-gather.1 = bf16[512,64]{0,1:T(8,128)(2,1)S(1)} all-gather(bf16[128,64]{0,1:T(8,128)(2,1)S(1)} %slice.9333), channel_id=3, replica_groups=mesh['blk'=64,'pair'=4] {'pair'}, dimensions={0}, use_global_device_ids=true | all-gather | bytes 81920 | tf_op jit(solution)/shard_map/all_gather | solution.py:101
  131.0 0.0 all-gather.4.cloned.1.call-done
  131.0 1.3 fusion.44
  138.6 2.7 %convolution_bitcast_fusion.1 = f32[1,128,64,128]{3,2,1,0:T(8,128)} fusion(bf16[128,128,128]{2,0,1:T(8,128)(2,1)S(1)} %constant_dynamic-update-slice_fusion.896, bf16[512,64]{0,1:T(8,128)(2,1)S(1)} %all-gather.1), kind=kOutput, calls=%fused_computation.16 | convolution fusion | flops 268435456 | bytes 8404992 | tf_op jit(solution)/shard_map/tk,tjr->jkr/dot_general | solution.py:111
  141.3 2.6 %convolution_bitcast_fusion.2 = f32[1,128,64,128]{3,2,1,0:T(8,128)} fusion(bf16[128,128,128]{2,0,1:T(8,128)(2,1)S(1)} %constant_dynamic-update-slice_fusion.768, bf16[512,64]{0,1:T(8,128)(2,1)S(1)} %all-gather.1), kind=kOutput, calls=%fused_computation.17 | convolution fusion | flops 268435456 | bytes 8404992 | tf_op jit(solution)/shard_map/tk,tjr->jkr/dot_general | solution.py:111
  147.0 2.7 %convolution_bitcast_fusion.3 = f32[1,128,64,128]{3,2,1,0:T(8,128)} fusion(bf16[128,128,128]{2,0,1:T(8,128)(2,1)S(1)} %constant_dynamic-update-slice_fusion.640, bf16[512,64]{0,1:T(8,128)(2,1)S(1)} %all-gather.1), kind=kOutput, calls=%fused_computation.18 | convolution fusion | flops 268435456 | bytes 8404992 | tf_op jit(solution)/shard_map/tk,tjr->jkr/dot_general | solution.py:111
  152.2 0.4 constant_dynamic-update-slice_fusion.532
  153.1 2.7 %convolution_bitcast_fusion.4 = f32[1,128,64,128]{3,2,1,0:T(8,128)} fusion(bf16[128,128,128]{2,0,1:T(8,128)(2,1)S(1)} %constant_dynamic-update-slice_fusion.512, bf16[512,64]{0,1:T(8,128)(2,1)S(1)} %all-gather.1), kind=kOutput, calls=%fused_computation.19 | convolution fusion | flops 268435456 | bytes 8404992 | tf_op jit(solution)/shard_map/tk,tjr->jkr/dot_general | solution.py:111
  158.8 2.7 %convolution_bitcast_fusion.5 = f32[1,128,64,128]{3,2,1,0:T(8,128)} fusion(bf16[128,128,128]{2,0,1:T(8,128)(2,1)S(1)} %constant_dynamic-update-slice_fusion.384, bf16[512,64]{0,1:T(8,128)(2,1)S(1)} %all-gather.1), kind=kOutput, calls=%fused_computation.20 | convolution fusion | flops 268435456 | bytes 8404992 | tf_op jit(solution)/shard_map/tk,tjr->jkr/dot_general | solution.py:111
  164.5 2.6 %convolution_bitcast_fusion.6 = f32[1,128,64,128]{3,2,1,0:T(8,128)} fusion(bf16[128,128,128]{2,0,1:T(8,128)(2,1)S(1)} %constant_dynamic-update-slice_fusion.256, bf16[512,64]{0,1:T(8,128)(2,1)S(1)} %all-gather.1), kind=kOutput, calls=%fused_computation.21 | convolution fusion | flops 268435456 | bytes 8404992 | tf_op jit(solution)/shard_map/tk,tjr->jkr/dot_general | solution.py:111
  170.2 2.7 %convolution_bitcast_fusion.7 = f32[1,128,64,128]{3,2,1,0:T(8,128)} fusion(bf16[128,128,128]{2,0,1:T(8,128)(2,1)S(1)} %constant_dynamic-update-slice_fusion.128, bf16[512,64]{0,1:T(8,128)(2,1)S(1)} %all-gather.1), kind=kOutput, calls=%fused_computation.22 | convolution fusion | flops 268435456 | bytes 8404992 | tf_op jit(solution)/shard_map/tk,tjr->jkr/dot_general | solution.py:111
  174.5 0.2 constant_dynamic-update-slice_fusion.60
  176.1 2.7 %convolution_bitcast_fusion.8 = f32[1,128,64,128]{3,2,1,0:T(8,128)} fusion(bf16[128,128,128]{2,0,1:T(8,128)(2,1)S(1)} %constant_dynamic-update-slice_fusion, bf16[512,64]{0,1:T(8,128)(2,1)S(1)} %all-gather.1), kind=kOutput, calls=%fused_computation.23 | convolution fusion | flops 268435456 | bytes 8404992 | tf_op jit(solution)/shard_map/tk,tjr->jkr/dot_general | solution.py:111
  178.8 0.0 copy-start.1
  178.8 16.4 %fusion.2 = f32[1,256,64,128]{3,2,1,0:T(8,128)} fusion(f32[1,128,64,128]{3,2,1,0:T(8,128)} %convolution_bitcast_fusion.7, f32[1,128,64,128]{3,2,1,0:T(8,128)} %convolution_bitcast_fusion.8, f32[1,128,64,128]{3,2,1,0:T(8,128)} %convolution_bitcast_fusion.5, f32[1,128,64,128]{3,2,1,0:T(8,128)} %convolution_bitcast_fusion.6, ...), kind=kLoop, calls=%fused_computation.5 | loop fusion | flops 16777216 | bytes 41975808 | tf_op jit(solution)/shard_map/mul | solution.py:120
  195.3 0.0 copy-done.1
  (1035 shorter events, 20.3 us)
Async XLA Ops:
  6.5 8.4 %copy-start = (bf16[64]{0:T(256)(128)(2,1)S(1)}, bf16[64]{0:T(256)(128)(2,1)}, u32[]{:S(2)}) copy-start(bf16[64]{0:T(256)(128)(2,1)} %param.7) | copy-start | bytes 388
  7.8 28.5 %collective-permute-start = (bf16[32,8192]{1,0:T(8,128)(2,1)S(1)}, bf16[32,8192]{1,0:T(8,128)(2,1)S(1)}, u32[]{:S(2)}, u32[]{:S(2)}) collective-permute-start(bf16[32,8192]{1,0:T(8,128)(2,1)S(1)} %get-tuple-element.5), channel_id=1, source_target_pairs={{0,4},{4,8},{8,12},{12,16},{16,20},{20,24},{24,28},{28,32},{32,36}... | collective-permute-start | bytes 1572872 | tf_op jit(solution)/shard_map/ppermute | solution.py:22
  12.8 23.6 %collective-permute-start.1 = (bf16[32,8192]{1,0:T(8,128)(2,1)S(1)}, bf16[32,8192]{1,0:T(8,128)(2,1)S(1)}, u32[]{:S(2)}, u32[]{:S(2)}) collective-permute-start(bf16[32,8192]{1,0:T(8,128)(2,1)S(1)} %get-tuple-element.6), channel_id=1, source_target_pairs={{4,0},{8,4},{12,8},{16,12},{20,16},{24,20},{28,24},{32,28},{36,32}... | collective-permute-start | bytes 1572872 | tf_op jit(solution)/shard_map/ppermute | solution.py:24
  36.4 17.0 %copy-start.3 = (bf16[255]{0:T(256)(128)(2,1)S(1)}, bf16[255]{0:T(256)(128)(2,1)}, u32[]{:S(2)}) copy-start(bf16[255]{0:T(256)(128)(2,1)} %param.8) | copy-start | bytes 1534
  39.8 50.3 %all-to-all-start = ((bf16[18,64,128]{2,0,1:T(8,128)(2,1)}), bf16[18,64,128]{2,0,1:T(8,128)(2,1)S(1)}, u32[]{:S(2)}, u32[]{:S(2)}) async-start(bf16[18,64,128]{2,0,1:T(8,128)(2,1)} %copy.12), calls=%async_computation | async-start | bytes 786432 | tf_op jit(solution)/shard_map/all_to_all | solution.py:62
  52.8 78.1 %all-gather.4.cloned.1.call-start = ((), (), s32[]{:S(2)}) async-start(), calls=%async_computation.2 | async-start | bytes 1474560 | tf_op jit(solution)/shard_map/all_gather | solution.py:100
  76.8 13.2 %copy-start.2 = (s32[64,64]{1,0:T(8,128)S(1)}, s32[64,64]{1,0:T(8,128)}, u32[]{:S(2)}) copy-start(s32[64,64]{1,0:T(8,128)} %param.9) | copy-start | bytes 49156
  90.0 19.0 %copy-start.4 = (s32[1,64]{1,0:T(1,128)S(1)}, s32[1,64]{1,0:T(1,128)}, u32[]{:S(2)}) copy-start(s32[1,64]{1,0:T(1,128)} %param.11) | copy-start | bytes 772
  90.0 19.1 %copy-start.5 = (s32[1,64]{1,0:T(1,128)S(1)}, s32[1,64]{1,0:T(1,128)}, u32[]{:S(2)}) copy-start(s32[1,64]{1,0:T(1,128)} %param.10) | copy-start | bytes 772
  98.6 23.0 %all-to-all-start.1 = ((bf16[64,2,1152]{2,1,0:T(2,128)(2,1)}), bf16[64,2,1152]{2,1,0:T(2,128)(2,1)S(1)}, u32[]{:S(2)}, u32[]{:S(2)}) async-start(bf16[64,2,1152]{2,1,0:T(2,128)(2,1)} %copy.14), calls=%async_computation.1 | async-start | bytes 589824 | tf_op jit(solution)/shard_map/all_to_all | solution.py:84
  178.8 16.4 %copy-start.1 = (bf16[64]{0:T(256)(128)(2,1)S(1)}, bf16[64]{0:T(256)(128)(2,1)}, u32[]{:S(2)}) copy-start(bf16[64]{0:T(256)(128)(2,1)} %param.7) | copy-start | bytes 388
Sparse Core Ops, SparseCore 0:
  93.7 26.9 all-gather.3
where the time goes:
time: 206 us; the launch traced here: 202 us
  local copies, waits for them, and re-layouts  83.7 us (41%)
  starting transfers between devices  30.8 us (15%)
  matrix products  29.4 us (14%)
  other arithmetic  18.6 us (9%)
  between operations  18.3 us (9%)
  waiting for transfers between devices  12.5 us (6%)
  blocking collectives  9.04 us (4%)
    gather x2, local copies, waits for them, and re-layouts, body(): aa_taps[jnp.clip(offset, 0, KA - 1)]  21.5 us
    dot_general x8, matrix products, body(): jnp.einsum('tk,tjr->jkr', sources_in[segment], hankel, preferred_element_...  21.4 us
    unnamed x1029, local copies, waits for them, and re-layouts  20.7 us
    another operation x2, local copies, waits for them, and re-layouts, whiten_matrix(): tiled = jnp.tile(rolled, length)[:length * (2 * length - 2)]  17.5 us
    mul x1, other arithmetic, body(): return (total * mask[None])[None]  16.4 us
    reshape x1, local copies, waits for them, and re-layouts, whiten_matrix(): return tiled.reshape(length, 2 * length - 2)[:, :length]  13.2 us
    all_to_all x1, starting transfers between devices, body(): lax.all_to_all(decimated, 'blk', split_axis=1, concat_axis=0, tiled=True)  13.1 us
    all_to_all x1, waiting for transfers between devices, body(): lax.all_to_all(outgoing, 'blk', split_axis=0, concat_axis=0, tiled=True)  12.5 us
  transfers between devices with their start and end apart: 5, of which 1 were waited for; matrix products, arithmetic and copies ran while one was open for 32% of the time, Pallas kernels for 0%

commit v1 on v0

v1 whole, which is shorter than its diff:
```python
import math

import jax
import jax.numpy as jnp
from jax import lax
from jax.experimental import pallas as pl
from jax.experimental.pallas import tpu as pltpu
from jax.sharding import PartitionSpec as P

DECIM = 8
KA = 64
LAGS = 1024
BLOCK = 128
LAG_GROUP = 64
STEP_LAGS = 8


def dot(a, b, contract=((1,), (0,))):
    return lax.dot_general(a, b, (contract, ((), ())), preferred_element_type=jnp.float32)


def decimation_matrix(aa_taps, before, rows, raw_len):
    out_rows = jnp.arange(rows)[:, None] - before
    offset = jnp.arange(raw_len)[None, :] - DECIM * out_rows + KA // 2
    hit = offset[:, :, None] == jnp.arange(KA)[None, None, :]
    picked = jnp.where(hit, aa_taps.astype(jnp.float32)[None, None, :], 0.0)
    return jnp.sum(picked, axis=2).astype(aa_taps.dtype)


def whiten_kernel(span, n_pairs, dec_ref, taps_ref, src_ref, win_ref, out_ref, white_ref):
    n_blocks = dec_ref.shape[0] // BLOCK
    tile = dec_ref.shape[1]
    toeplitz = pltpu.roll(
        jnp.broadcast_to(taps_ref[...], (BLOCK, 3 * BLOCK)), 1, 1, stride=1, stride_axis=0
    ).astype(jnp.bfloat16)
    for block in range(n_blocks):
        low = max(block - 1, 0)
        high = min(block + 2, n_blocks)
        skip = (low - block + 1) * BLOCK
        rows = (high - low) * BLOCK
        white_ref[block * BLOCK : (block + 1) * BLOCK, :] = dot(
            toeplitz[:, skip : skip + rows], dec_ref[low * BLOCK : high * BLOCK, :]
        ).astype(jnp.bfloat16)
    share = LAGS // n_pairs
    for pair in range(n_pairs):
        win_ref[pair] = white_ref[pair * share : pair * share + share + span, :]
    mine = lax.axis_index("blk")
    src = src_ref[...]
    belongs = (src // tile) == mine
    chan = src - mine * tile
    first = jnp.min(jnp.where(belongs, chan, tile), axis=1, keepdims=True)
    last = jnp.max(jnp.where(belongs, chan, -1), axis=1, keepdims=True)
    lane = lax.broadcasted_iota(jnp.int32, (src.shape[0], tile), 1)
    source_time = white_ref[LAGS // 2 : LAGS // 2 + span, :]
    for slot, channel in enumerate((first, last)):
        picker = jnp.where(lane == channel, 1.0, 0.0).astype(jnp.bfloat16)
        out_ref[slot] = dot(picker, source_time, ((1,), (1,))).astype(jnp.bfloat16)


def correlate_kernel(span, n_src, got_ref, low_ref, high_ref, out_ref, lhs_ref, rhs_ref, src_ref):
    step = pl.program_id(0)
    segments, _, tile = got_ref.shape
    groups = out_ref.shape[0]
    reach = span + LAG_GROUP
    window = groups * LAG_GROUP + span

    @pl.when(step == 0)
    def _():
        gap = jnp.zeros((n_src, LAG_GROUP), jnp.float32)
        pieces = []
        for seg in range(segments):
            pieces += [got_ref[seg, window : window + n_src, :].astype(jnp.float32), gap]
            for group in range(groups):
                rhs_ref[seg * reach : (seg + 1) * reach, group * tile : (group + 1) * tile] = got_ref[
                    seg, group * LAG_GROUP : group * LAG_GROUP + reach, :
                ]
        src_ref[...] = jnp.concatenate(pieces, axis=1)

    base = src_ref[...]
    for lag in range(STEP_LAGS):
        rolled = pltpu.roll(base, lag, 1) if lag else base
        lhs_ref[lag * n_src : (lag + 1) * n_src, :] = rolled.astype(jnp.bfloat16)
    src_ref[...] = pltpu.roll(base, STEP_LAGS, 1)
    scale = 1.0 / math.sqrt(span * segments)
    position = lax.broadcasted_iota(jnp.int32, (n_src, tile), 1)
    inside = (position >= low_ref[...]) & (position < high_ref[...])
    mask = jnp.where(inside, jnp.float32(scale), jnp.float32(0.0))
    for group in range(0, groups, 2):
        product = dot(lhs_ref[...], rhs_ref[:, group * tile : (group + 2) * tile])
        for half in range(2):
            piece = product[:, half * tile : (half + 1) * tile].reshape(STEP_LAGS, n_src, tile)
            out_ref[group + half] = jnp.where(inside[None], piece * mask[None], 0.0)


def body(raw_strain, aa_taps, white_taps, src_channels, recv_lo, recv_hi):
    raw_len = raw_strain.shape[1]
    short_len = raw_len // DECIM
    channels = raw_strain.shape[2]
    n_blocks = lax.axis_size("blk")
    n_pairs = lax.axis_size("pair")
    tile = channels // n_blocks
    seg_len = short_len * n_blocks
    span = seg_len - LAGS
    n_src = src_channels.shape[1]
    n_tiles = src_channels.shape[0]
    share = LAGS // n_pairs

    before = KA // 2 // DECIM - 1
    after = KA // 2 // DECIM
    matrix = decimation_matrix(aa_taps, before, before + short_len + after, raw_len)
    partial = dot(matrix, raw_strain[0])
    ends = n_blocks - 1
    from_next = lax.ppermute(partial[:before], "blk", [(i + 1, i) for i in range(ends)])
    from_last = lax.ppermute(partial[before + short_len :], "blk", [(i, i + 1) for i in range(ends)])
    own = partial[before : before + short_len]
    decimated = jnp.concatenate(
        [
            own[:after] + from_last,
            own[after : short_len - before],
            own[short_len - before :] + from_next,
        ],
        axis=0,
    ).astype(jnp.bfloat16)
    tile_dec = lax.all_to_all(decimated, "blk", split_axis=1, concat_axis=0, tiled=True)

    taps = jnp.pad(white_taps.astype(jnp.float32), (0, 3 * BLOCK - white_taps.shape[0]))[None]
    windows, outgoing = pl.pallas_call(
        lambda *refs: whiten_kernel(span, n_pairs, *refs),
        out_shape=(
            jax.ShapeDtypeStruct((n_pairs, share + span, tile), jnp.bfloat16),
            jax.ShapeDtypeStruct((2, n_tiles, span), jnp.bfloat16),
        ),
        scratch_shapes=[pltpu.VMEM((seg_len, tile), jnp.bfloat16)],
        name="whiten",
    )(tile_dec, taps, src_channels)
    incoming = lax.all_to_all(outgoing, "blk", split_axis=1, concat_axis=1, tiled=True)
    own_src = lax.dynamic_index_in_dim(src_channels, lax.axis_index("blk"), 0, keepdims=False)
    own_tile = own_src // tile
    is_last = jnp.any(
        (own_tile[:, None] == own_tile[None, :]) & (own_src[None, :] < own_src[:, None]), axis=1
    )
    place = own_tile + jnp.where(is_last, n_tiles, 0)
    selector = (place[:, None] == jnp.arange(2 * n_tiles)[None, :]).astype(jnp.bfloat16)
    sources = dot(selector, incoming.reshape(2 * n_tiles, span)).astype(jnp.bfloat16)
    parcel = jnp.concatenate(
        [windows, jnp.broadcast_to(sources[None], (n_pairs, n_src, span))], axis=1
    )
    got = lax.all_to_all(parcel, "pair", split_axis=0, concat_axis=0, tiled=True)

    groups = share // LAG_GROUP
    reach = n_pairs * (span + LAG_GROUP)
    whole = lambda *shape: pl.BlockSpec(shape, lambda i: (0,) * len(shape))
    xcorr = pl.pallas_call(
        lambda *refs: correlate_kernel(span, n_src, *refs),
        grid=(LAG_GROUP // STEP_LAGS,),
        in_specs=[whole(*got.shape), whole(n_src, 1), whole(n_src, 1)],
        out_specs=pl.BlockSpec((groups, STEP_LAGS, n_src, tile), lambda i: (0, i, 0, 0)),
        out_shape=jax.ShapeDtypeStruct((groups, LAG_GROUP, n_src, tile), jnp.float32),
        scratch_shapes=[
            pltpu.VMEM((STEP_LAGS * n_src, reach), jnp.bfloat16),
            pltpu.VMEM((reach, groups * tile), jnp.bfloat16),
            pltpu.VMEM((n_src, reach), jnp.float32),
        ],
        name="correlate",
    )(got, recv_lo.reshape(n_src, 1), recv_hi.reshape(n_src, 1))
    return xcorr.reshape(1, share, n_src, tile)


def solution(mesh):
    placed = (P("pair", "blk", None), P(), P(), P(), P("blk", None), P("blk", None))
    return jax.shard_map(
        body, mesh=mesh, in_specs=placed, out_specs=P("blk", "pair", None, None), check_vma=False
    )
```

time: 206 us -> 83.4 us (0.40); the launches traced: 202 us -> 82.9 us
  local copies, waits for them, and re-layouts: 83.7 us -> 5.69 us
  matrix products: 29.4 us -> 0.64 us
  between operations: 18.3 us -> 0.15 us
  waiting for transfers between devices: 12.5 us -> 29.4 us
  other arithmetic: 18.6 us -> 5.73 us
  Pallas kernels: 0 us -> 10.4 us
  blocking collectives: 9.04 us -> 0 us
    dot_general x13 -> x2, matrix products: 29.4 us -> 0.64 us  [dot(): lax.dot_general(a, b, (contract, ((), ())), preferred_element_type=jnp.fl...]
    gather x2 -> x0, local copies, waits for them, and re-layouts: 21.5 us -> none  [body(): aa_taps[jnp.clip(offset, 0, KA - 1)]]
    unnamed x1029 -> x11, local copies, waits for them, and re-layouts: 20.7 us -> 1.22 us
    another operation x10 -> x0, local copies, waits for them, and re-layouts: 17.7 us -> none  [the longest x2 17.5 us: whiten_matrix(): tiled = jnp.tile(rolled, length)[:length * (2 * length - 2)]]
    mul x2 -> x1, other arithmetic: 16.4 us -> 0.01 us  [decimation_matrix(): offset = jnp.arange(raw_len)[None, :] - DECIM * out_rows + KA // 2]
    all_to_all x1, waiting for transfers between devices: 0.01 us -> 12.4 us  [body(): lax.all_to_all(decimated, 'blk', split_axis=1, concat_axis=0, tiled=True)]
    reshape x1 -> x2, local copies, waits for them, and re-layouts: 13.2 us -> 1.39 us  [the longest x1 0.7 us: body(): recv_lo.reshape(n_src, 1)]
    pallas_call x0 -> x2, Pallas kernels: none -> 10.4 us  [the longest x1 8.15 us: body(): pl.pallas_call(lambda *refs: correlate_kernel(span, n_src, *refs), grid=(...]
  transfers between devices with their start and end apart: 5 -> 5, of which waited for: 1 -> 5; matrix products, arithmetic and copies ran while one was open for 32% -> 5% of each run, Pallas kernels for 0% -> 0%
where the time goes in v1:
time: 83.4 us; the launch traced here: 82.9 us
  starting transfers between devices  30.9 us (37%)
  waiting for transfers between devices  29.4 us (35%)
  Pallas kernels  10.4 us (12%)
  other arithmetic  5.73 us (7%)
  local copies, waits for them, and re-layouts  5.69 us (7%)
    all_to_all x1, starting transfers between devices, body(): lax.all_to_all(decimated, 'blk', split_axis=1, concat_axis=0, tiled=True)  13.6 us
    all_to_all x1, waiting for transfers between devices, body(): lax.all_to_all(decimated, 'blk', split_axis=1, concat_axis=0, tiled=True)  12.4 us
    all_to_all x1, waiting for transfers between devices, body(): lax.all_to_all(outgoing, 'blk', split_axis=1, concat_axis=1, tiled=True)  9.2 us
    pallas_call x1, Pallas kernels, body(): pl.pallas_call(lambda *refs: correlate_kernel(span, n_src, *refs), grid=(...  8.15 us
    all_to_all x1, starting transfers between devices, body(): lax.all_to_all(outgoing, 'blk', split_axis=1, concat_axis=1, tiled=True)  6.21 us
    all_to_all x1, waiting for transfers between devices, body(): lax.all_to_all(parcel, 'pair', split_axis=0, concat_axis=0, tiled=True)  6.18 us
    ppermute x1, starting transfers between devices, body(): lax.ppermute(partial[:before], 'blk', [(i + 1, i) for i in range(ends)])  5.15 us
    all_to_all x1, starting transfers between devices, body(): lax.all_to_all(parcel, 'pair', split_axis=0, concat_axis=0, tiled=True)  4 us
  transfers between devices with their start and end apart: 5, of which 5 were waited for; matrix products, arithmetic and copies ran while one was open for 5% of the time, Pallas kernels for 0%

profile of v1, /device:TPU:1, one launch (start us, length us, event | category | flops | bytes accessed | tf_op | source)
XLA Modules:
  0.0 82.9 jit_solution(13998872485527585022)
XLA Ops:
  0.0 0.0 copy-start
  0.0 0.8 convert_element_type.15
  0.8 0.1 subtract_add_fusion
  0.9 0.4 select_reduce_fusion
  1.3 0.4 copy-done
  1.7 0.4 fusion
  2.1 0.0 copy-start.4
  2.2 5.1 %collective-permute-start.1 = (f32[3,8192]{1,0:T(4,128)S(1)}, f32[3,8192]{1,0:T(4,128)S(1)}, u32[]{:S(2)}, u32[]{:S(2)}) collective-permute-start(f32[3,8192]{1,0:T(4,128)S(1)} %slice.29), channel_id=1, source_target_pairs={{4,0},{8,4},{12,8},{16,12},{20,16},{24,20},{28,24},{32,28},{36,32}... | collective-permute-start | bytes 294920 | tf_op jit(solution)/shard_map/ppermute | solution.py:113
  7.4 1.9 %collective-permute-start = (f32[4,8192]{1,0:T(4,128)S(1)}, f32[4,8192]{1,0:T(4,128)S(1)}, u32[]{:S(2)}, u32[]{:S(2)}) collective-permute-start(f32[4,8192]{1,0:T(4,128)S(1)} %slice.26), channel_id=1, source_target_pairs={{0,4},{4,8},{8,12},{12,16},{16,20},{20,24},{24,28},{28,32},{32,36}... | collective-permute-start | bytes 393224 | tf_op jit(solution)/shard_map/ppermute | solution.py:114
  9.4 0.1 copy.31
  9.6 0.2 collective-permute-done.1
  9.8 1.4 %collective-permute-done = f32[4,8192]{1,0:T(4,128)S(1)} collective-permute-done((f32[4,8192]{1,0:T(4,128)S(1)}, f32[4,8192]{1,0:T(4,128)S(1)}, u32[]{:S(2)}, u32[]{:S(2)}) %collective-permute-start) | collective-permute-done | bytes 131104 | tf_op jit(solution)/shard_map/ppermute | solution.py:114
  11.3 0.0 copy-start.2
  11.3 0.0 copy-start.3
  11.3 1.0 %pad_maximum_fusion.1 = bf16[18,64,128]{2,0,1:T(8,128)(2,1)} fusion(bf16[3,64,128]{2,0,1:T(4,128)(2,1)S(1)} %fusion.5, bf16[11,64,128]{2,0,1:T(8,128)(2,1)S(1)} %copy.31, bf16[4,64,128]{2,0,1:T(4,128)(2,1)S(1)} %fusion.4), kind=kLoop, calls=%fused_computation.7 | loop fusion | flops 884736 | bytes 589824 | tf_op jit(solution)/shard_map/concatenate | solution.py:116
  12.3 13.6 %all-to-all-start = ((bf16[18,64,128]{2,0,1:T(8,128)(2,1)}), bf16[18,64,128]{2,0,1:T(8,128)(2,1)S(1)}, u32[]{:S(2)}, u32[]{:S(2)}) async-start(bf16[18,64,128]{2,0,1:T(8,128)(2,1)} %pad_maximum_fusion.1), calls=%async_computation | async-start | bytes 786432 | tf_op jit(solution)/shard_map/all_to_all | solution.py:124
  25.8 0.0 copy-done.4
  25.9 0.6 reshape.98.refs_1_
  26.5 0.7 fusion.8
  27.2 0.7 and_select_fusion.1
  27.9 0.2 and_reduce_fusion
  28.0 12.4 %all-to-all-done = bf16[18,64,128]{2,0,1:T(8,128)(2,1)S(1)} async-done(((bf16[18,64,128]{2,0,1:T(8,128)(2,1)}), bf16[18,64,128]{2,0,1:T(8,128)(2,1)S(1)}, u32[]{:S(2)}, u32[]{:S(2)}) %all-to-all-start) | async-done | bytes 294944 | tf_op jit(solution)/shard_map/all_to_all | solution.py:124
  40.5 0.8 all_to_all.20.refs_0_
  41.3 2.3 %whiten.1 = (bf16[4,384,128]{2,1,0:T(8,128)(2,1)}, bf16[2,64,128]{2,1,0:T(8,128)(2,1)}) custom-call(bf16[1152,128]{1,0:T(8,128)(2,1)} %all_to_all.20.refs_0_, f32[1,384]{1,0:T(1,128)} %reshape.98.refs_1_, s32[64,64]{1,0:T(8,128)} %refs_2_.1), custom_call_target="tpu_custom_call" | custom-call | tf_op jit(solution)/shard_map/whiten/pallas_call | solution.py:127
  43.5 1.4 %copy.33 = bf16[2,64,128]{2,0,1:T(2,128)(2,1)} copy(bf16[2,64,128]{2,1,0:T(8,128)(2,1)} %get-tuple-element.8) | data formatting | bytes 65536 | tf_op jit(solution)/shard_map/whiten/pallas_call | solution.py:127
  44.9 6.2 %all-to-all-start.1 = ((bf16[2,64,128]{2,0,1:T(2,128)(2,1)}), bf16[2,64,128]{2,0,1:T(2,128)(2,1)S(1)}, u32[]{:S(2)}, u32[]{:S(2)}) async-start(bf16[2,64,128]{2,0,1:T(2,128)(2,1)} %copy.33), calls=%async_computation.1 | async-start | bytes 65536 | tf_op jit(solution)/shard_map/all_to_all | solution.py:136
  51.2 9.2 %all-to-all-done.1 = bf16[2,64,128]{2,0,1:T(2,128)(2,1)S(1)} async-done(((bf16[2,64,128]{2,0,1:T(2,128)(2,1)}), bf16[2,64,128]{2,0,1:T(2,128)(2,1)S(1)}, u32[]{:S(2)}, u32[]{:S(2)}) %all-to-all-start.1) | async-done | bytes 32800 | tf_op jit(solution)/shard_map/all_to_all | solution.py:136
  60.4 0.2 convolution_convert_fusion
  60.6 1.8 %pad_maximum_fusion = bf16[4,448,128]{2,1,0:T(8,128)(2,1)} fusion(bf16[4,64,128]{2,1,0:T(8,128)(2,1)S(1)} %broadcast_in_dim.45, bf16[4,384,128]{2,1,0:T(8,128)(2,1)} %get-tuple-element.7), kind=kLoop, calls=%fused_computation.6 | loop fusion | flops 917504 | bytes 917504 | tf_op jit(solution)/shard_map/concatenate | solution.py:145
  62.4 4.0 %all-to-all-start.2 = ((bf16[4,448,128]{2,1,0:T(8,128)(2,1)}), bf16[4,448,128]{2,1,0:T(8,128)(2,1)S(1)}, u32[]{:S(2)}, u32[]{:S(2)}) async-start(bf16[4,448,128]{2,1,0:T(8,128)(2,1)} %pad_maximum_fusion), calls=%async_computation.2 | async-start | bytes 917504 | tf_op jit(solution)/shard_map/all_to_all | solution.py:148
  66.4 0.0 copy-done.2
  66.4 0.7 copy.35.refs_1_
  67.1 0.0 copy-done.3
  67.1 0.7 copy.36.refs_2_
  67.8 6.2 %all-to-all-done.2.refs_0_ = bf16[4,448,128]{2,1,0:T(8,128)(2,1)S(1)} async-done(((bf16[4,448,128]{2,1,0:T(8,128)(2,1)}), bf16[4,448,128]{2,1,0:T(8,128)(2,1)S(1)}, u32[]{:S(2)}, u32[]{:S(2)}) %all-to-all-start.2) | async-done | bytes 458784 | tf_op jit(solution)/shard_map/all_to_all | solution.py:148
  74.0 0.0 copy-start.1
  74.0 0.8 copy-done.1
  74.7 8.1 %correlate.1 = f32[4,64,64,128]{3,2,1,0:T(8,128)} custom-call(bf16[4,448,128]{2,1,0:T(8,128)(2,1)} %copy-done.1, s32[64,1]{1,0:T(8,128)} %copy.35.refs_1_, s32[64,1]{1,0:T(8,128)} %copy.36.refs_2_), custom_call_target="tpu_custom_call" | custom-call | tf_op jit(solution)/shard_map/correlate/pallas_call | solution.py:153
  (12 shorter events, 0.3 us)
Async XLA Ops:
  0.0 1.7 %copy-start = (bf16[1,144,8192]{2,1,0:T(8,128)(2,1)S(1)}, bf16[1,144,8192]{2,1,0:T(8,128)(2,1)}, u32[]{:S(2)}) copy-start(bf16[1,144,8192]{2,1,0:T(8,128)(2,1)} %param.6) | copy-start | bytes 7077892
  2.1 23.7 %copy-start.4 = (bf16[255]{0:T(256)(128)(2,1)S(1)}, bf16[255]{0:T(256)(128)(2,1)}, u32[]{:S(2)}) copy-start(bf16[255]{0:T(256)(128)(2,1)} %param.8) | copy-start | bytes 1534
  2.2 7.6 %collective-permute-start.1 = (f32[3,8192]{1,0:T(4,128)S(1)}, f32[3,8192]{1,0:T(4,128)S(1)}, u32[]{:S(2)}, u32[]{:S(2)}) collective-permute-start(f32[3,8192]{1,0:T(4,128)S(1)} %slice.29), channel_id=1, source_target_pairs={{4,0},{8,4},{12,8},{16,12},{20,16},{24,20},{28,24},{32,28},{36,32}... | collective-permute-start | bytes 294920 | tf_op jit(solution)/shard_map/ppermute | solution.py:113
  7.4 3.9 %collective-permute-start = (f32[4,8192]{1,0:T(4,128)S(1)}, f32[4,8192]{1,0:T(4,128)S(1)}, u32[]{:S(2)}, u32[]{:S(2)}) collective-permute-start(f32[4,8192]{1,0:T(4,128)S(1)} %slice.26), channel_id=1, source_target_pairs={{0,4},{4,8},{8,12},{12,16},{16,20},{20,24},{24,28},{28,32},{32,36}... | collective-permute-start | bytes 393224 | tf_op jit(solution)/shard_map/ppermute | solution.py:114
  11.3 55.1 %copy-start.2 = (s32[1,64]{1,0:T(1,128)S(1)}, s32[1,64]{1,0:T(1,128)}, u32[]{:S(2)}) copy-start(s32[1,64]{1,0:T(1,128)} %param.10) | copy-start | bytes 772
  11.3 55.8 %copy-start.3 = (s32[1,64]{1,0:T(1,128)S(1)}, s32[1,64]{1,0:T(1,128)}, u32[]{:S(2)}) copy-start(s32[1,64]{1,0:T(1,128)} %param.11) | copy-start | bytes 772
  12.3 28.2 %all-to-all-start = ((bf16[18,64,128]{2,0,1:T(8,128)(2,1)}), bf16[18,64,128]{2,0,1:T(8,128)(2,1)S(1)}, u32[]{:S(2)}, u32[]{:S(2)}) async-start(bf16[18,64,128]{2,0,1:T(8,128)(2,1)} %pad_maximum_fusion.1), calls=%async_computation | async-start | bytes 786432 | tf_op jit(solution)/shard_map/all_to_all | solution.py:124
  44.9 15.4 %all-to-all-start.1 = ((bf16[2,64,128]{2,0,1:T(2,128)(2,1)}), bf16[2,64,128]{2,0,1:T(2,128)(2,1)S(1)}, u32[]{:S(2)}, u32[]{:S(2)}) async-start(bf16[2,64,128]{2,0,1:T(2,128)(2,1)} %copy.33), calls=%async_computation.1 | async-start | bytes 65536 | tf_op jit(solution)/shard_map/all_to_all | solution.py:136
  62.4 11.6 %all-to-all-start.2 = ((bf16[4,448,128]{2,1,0:T(8,128)(2,1)}), bf16[4,448,128]{2,1,0:T(8,128)(2,1)S(1)}, u32[]{:S(2)}, u32[]{:S(2)}) async-start(bf16[4,448,128]{2,1,0:T(8,128)(2,1)} %pad_maximum_fusion), calls=%async_computation.2 | async-start | bytes 917504 | tf_op jit(solution)/shard_map/all_to_all | solution.py:148
  74.0 0.8 copy-start.1

commit v2 on v1

v2 whole, which is shorter than its diff:
```python
import math

import jax
import jax.numpy as jnp
from jax import lax
from jax.experimental import pallas as pl
from jax.experimental.pallas import tpu as pltpu
from jax.sharding import PartitionSpec as P

DECIM = 8
KA = 64
LAGS = 1024
BLOCK = 128
LAG_GROUP = 64
STEP_LAGS = 8


def dot(a, b, contract=((1,), (0,))):
    return lax.dot_general(a, b, (contract, ((), ())), preferred_element_type=jnp.float32)


def rounded(value, unit):
    return -(-value // unit) * unit


def exchange_kernel(
    n_blk, n_pair, rows, span,
    raw_ref, aa_ref, taps_ref, src_ref, out_ref,
    own_ref, to_prev, to_next, from_prev, from_next, dec_ref, recv_ref,
    white_ref, offer_ref, taken_ref, pick_ref, got_ref, expand_ref,
    edge_send, edge_recv, dec_send, dec_recv, src_send, src_recv,
    win_send, win_recv, pick_send, pick_recv,
):
    me = lax.axis_index("blk")
    seg = lax.axis_index("pair")
    slot = dec_ref.shape[1]
    tile = dec_ref.shape[2]
    raw_len = raw_ref.shape[0]
    share = LAGS // n_pair
    window = share + span
    n_src = pick_ref.shape[0]
    edge = KA // 2 // DECIM

    recv_ref[...] = jnp.zeros(recv_ref.shape, recv_ref.dtype)
    barrier = pltpu.get_barrier_semaphore()

    def greet(step, carry):
        pl.semaphore_signal(barrier, inc=1, device_id={"blk": lax.rem(me + step, n_blk)})
        return carry

    lax.fori_loop(1, n_blk, greet, 0)
    for step in range(1, n_pair):
        pl.semaphore_signal(barrier, inc=1, device_id={"pair": lax.rem(seg + step, n_pair)})

    width = aa_ref.shape[1]
    lead = 2 * edge
    octets = []
    for start in range(0, rounded(lead + max(slot, rows + edge), 8), 8):
        shift = (DECIM * (start - lead) - KA // 2) % width
        shifted = pltpu.roll(jnp.broadcast_to(aa_ref[...], (8, width)), shift, 1)
        octets.append(pltpu.roll(shifted, 0, 1, stride=DECIM, stride_axis=0))
    matrix = jnp.concatenate(octets, axis=0)[:, :raw_len].astype(jnp.bfloat16)
    chunk = 8 * tile

    def decimate(index, carry):
        cols = pl.ds(pl.multiple_of(index * chunk, chunk), chunk)
        product = dot(matrix, raw_ref[:, cols])
        own_ref[:, cols] = product[lead : lead + slot]
        to_prev[:, cols] = product[lead - edge : lead]
        to_next[:, cols] = product[lead + rows : lead + rows + edge]
        return carry

    lax.fori_loop(0, n_blk // 8, decimate, 0)
    pl.semaphore_wait(barrier, n_blk - 1 + n_pair - 1)

    up = pltpu.make_async_remote_copy(
        to_next, from_prev, edge_send.at[0], edge_recv.at[0],
        device_id={"blk": lax.rem(me + 1, n_blk)},
    )
    down = pltpu.make_async_remote_copy(
        to_prev, from_next, edge_send.at[1], edge_recv.at[1],
        device_id={"blk": lax.rem(me + n_blk - 1, n_blk)},
    )
    up.start()
    down.start()

    period = 144 // rows
    depth = period * slot
    reach = taps_ref.shape[1]
    compact = pltpu.roll(
        jnp.broadcast_to(taps_ref[...], (144, reach)), 17, 1, stride=1, stride_axis=0
    ).astype(jnp.bfloat16)
    wide = lax.broadcasted_iota(jnp.int32, (reach, 3 * depth), 1)
    tall = lax.broadcasted_iota(jnp.int32, (reach, 3 * depth), 0)
    inner = lax.rem(wide, slot)
    hit = (tall == (wide // slot) * rows + inner) & (inner < rows)
    expand_ref[...] = dot(compact, jnp.where(hit, 1.0, 0.0).astype(jnp.bfloat16)).astype(
        jnp.bfloat16
    )

    up.wait()
    down.wait()

    def finish(index, carry):
        cols = pl.ds(pl.multiple_of(index * chunk, chunk), chunk)
        own_ref[0:edge, cols] += jnp.where(me > 0, from_prev[:, cols], 0.0)
        own_ref[rows - edge : rows, cols] += jnp.where(me < n_blk - 1, from_next[:, cols], 0.0)
        block = own_ref[:, cols].astype(jnp.bfloat16)
        for part in range(8):
            dec_ref[index * 8 + part] = block[:, part * tile : (part + 1) * tile]
        return carry

    lax.fori_loop(0, n_blk // 8, finish, 0)

    def block_copy(peer, place):
        return pltpu.make_async_remote_copy(
            dec_ref.at[peer, pl.ds(0, rows)], recv_ref.at[place, pl.ds(0, rows)],
            dec_send.at[peer], dec_recv.at[place], device_id={"blk": peer},
        )

    def send_block(step, carry):
        block_copy(lax.rem(me + step, n_blk), me).start()
        return carry

    def wait_block(step, carry):
        peer = lax.rem(me + step, n_blk)
        copy = block_copy(peer, peer)
        copy.wait_send()
        copy.wait_recv()
        return carry

    lax.fori_loop(1, n_blk, send_block, 0)
    recv_ref[me] = dec_ref[me]

    src = src_ref[...]
    belongs = (src // tile) == me
    chan = src - me * tile
    first = jnp.min(jnp.where(belongs, chan, tile), axis=1, keepdims=True)
    last = jnp.max(jnp.where(belongs, chan, -1), axis=1, keepdims=True)
    lane = lax.broadcasted_iota(jnp.int32, (n_blk, tile), 1)
    pickers = [
        jnp.where(lane == channel, 1.0, 0.0).astype(jnp.bfloat16) for channel in (first, last)
    ]
    row = src_ref[pl.ds(me, 1), :]
    square = (n_src, n_src)
    across = jnp.broadcast_to(row, square).astype(jnp.float32)
    diagonal = lax.broadcasted_iota(jnp.int32, square, 0) == lax.broadcasted_iota(
        jnp.int32, square, 1
    )
    column = jnp.sum(jnp.where(diagonal, across, 0.0), axis=1, keepdims=True)
    column = column.astype(jnp.int32)
    same = (row // tile) == (column // tile)
    later = jnp.max(jnp.where(same & (row < column), 1.0, 0.0), axis=1, keepdims=True)
    owner = lax.broadcasted_iota(jnp.int32, (n_src, n_blk), 1) == (column // tile)
    selectors = [
        jnp.where(owner & (later == float(which)), 1.0, 0.0).astype(jnp.bfloat16)
        for which in range(2)
    ]

    lax.fori_loop(1, n_blk, wait_block, 0)

    groups = n_blk // period
    for group in range(groups):
        low, high = max(group - 1, 0), min(group + 2, groups)
        skip = (low - group + 1) * depth
        held = recv_ref[low * period : high * period].reshape((high - low) * depth, tile)
        white_ref[group * 144 : (group + 1) * 144, :] = dot(
            expand_ref[:, skip : skip + (high - low) * depth], held
        ).astype(jnp.bfloat16)

    source_time = white_ref[LAGS // 2 : LAGS // 2 + span, :]
    for which in range(2):
        offer_ref[:, which, :] = dot(pickers[which], source_time, ((1,), (1,)))

    def source_copy(peer, place):
        return pltpu.make_async_remote_copy(
            offer_ref.at[peer], taken_ref.at[place],
            src_send.at[peer], src_recv.at[place], device_id={"blk": peer},
        )

    def send_source(step, carry):
        source_copy(lax.rem(me + step, n_blk), me).start()
        return carry

    def wait_source(step, carry):
        peer = lax.rem(me + step, n_blk)
        copy = source_copy(peer, peer)
        copy.wait_send()
        copy.wait_recv()
        return carry

    def window_copy(peer, place):
        return pltpu.make_async_remote_copy(
            white_ref.at[pl.ds(pl.multiple_of(peer * share, share), window)],
            got_ref.at[place, pl.ds(0, window)],
            win_send.at[peer], win_recv.at[place], device_id={"pair": peer},
        )

    def pick_copy(peer, place):
        return pltpu.make_async_remote_copy(
            pick_ref, got_ref.at[place, pl.ds(window, n_src)],
            pick_send.at[peer], pick_recv.at[place], device_id={"pair": peer},
        )

    pair_peers = [lax.rem(seg + step, n_pair) for step in range(1, n_pair)]
    lax.fori_loop(1, n_blk, send_source, 0)
    for peer in pair_peers:
        window_copy(peer, seg).start()
    taken_ref[me] = offer_ref[me]
    got_ref[seg, 0:window] = white_ref[pl.ds(pl.multiple_of(seg * share, share), window), :]
    lax.fori_loop(1, n_blk, wait_source, 0)
    picked = jnp.zeros((n_src, span), jnp.float32)
    for which in range(2):
        picked += dot(selectors[which], taken_ref[:, which, :].astype(jnp.bfloat16))
    pick_ref[...] = picked.astype(jnp.bfloat16)
    for peer in pair_peers:
        pick_copy(peer, seg).start()
    got_ref[seg, window : window + n_src] = picked.astype(jnp.bfloat16)
    for peer in pair_peers:
        for copy in (window_copy(peer, peer), pick_copy(peer, peer)):
            copy.wait_send()
            copy.wait_recv()
    out_ref[...] = got_ref[...]


def correlate_kernel(span, n_src, got_ref, low_ref, high_ref, out_ref, lhs_ref, rhs_ref, src_ref):
    step = pl.program_id(0)
    segments, _, tile = got_ref.shape
    groups = out_ref.shape[0]
    reach = span + LAG_GROUP
    window = groups * LAG_GROUP + span

    @pl.when(step == 0)
    def _():
        gap = jnp.zeros((n_src, LAG_GROUP), jnp.float32)
        pieces = []
        for seg in range(segments):
            pieces += [got_ref[seg, window : window + n_src, :].astype(jnp.float32), gap]
            for group in range(groups):
                rhs_ref[seg * reach : (seg + 1) * reach, group * tile : (group + 1) * tile] = got_ref[
                    seg, group * LAG_GROUP : group * LAG_GROUP + reach, :
                ]
        src_ref[...] = jnp.concatenate(pieces, axis=1)

    base = src_ref[...]
    for lag in range(STEP_LAGS):
        rolled = pltpu.roll(base, lag, 1) if lag else base
        lhs_ref[lag * n_src : (lag + 1) * n_src, :] = rolled.astype(jnp.bfloat16)
    src_ref[...] = pltpu.roll(base, STEP_LAGS, 1)
    scale = 1.0 / math.sqrt(span * segments)
    position = lax.broadcasted_iota(jnp.int32, (n_src, tile), 1)
    inside = (position >= low_ref[...]) & (position < high_ref[...])
    mask = jnp.where(inside, jnp.float32(scale), jnp.float32(0.0))
    for group in range(0, groups, 2):
        product = dot(lhs_ref[...], rhs_ref[:, group * tile : (group + 2) * tile])
        for half in range(2):
            piece = product[:, half * tile : (half + 1) * tile].reshape(STEP_LAGS, n_src, tile)
            out_ref[group + half] = jnp.where(inside[None], piece * mask[None], 0.0)


def body(raw_strain, aa_taps, white_taps, src_channels, recv_lo, recv_hi):
    raw_len = raw_strain.shape[1]
    short_len = raw_len // DECIM
    channels = raw_strain.shape[2]
    n_blocks = lax.axis_size("blk")
    n_pairs = lax.axis_size("pair")
    tile = channels // n_blocks
    seg_len = short_len * n_blocks
    span = seg_len - LAGS
    n_src = src_channels.shape[1]
    n_tiles = src_channels.shape[0]
    share = LAGS // n_pairs

    slot = rounded(short_len, 16)
    edge = KA // 2 // DECIM
    aa_width = rounded(DECIM * (slot + 3 * edge) + KA + KA // 2, BLOCK)
    aa_row = jnp.pad(aa_taps.astype(jnp.float32), (0, aa_width - KA))[None]
    taps = jnp.pad(white_taps.astype(jnp.float32), (0, 4 * BLOCK - white_taps.shape[0]))[None]
    depth = 144 // short_len * slot
    dma = pltpu.SemaphoreType.DMA
    vmem = pl.BlockSpec(memory_space=pltpu.VMEM)
    got = pl.pallas_call(
        lambda *refs: exchange_kernel(n_blocks, n_pairs, short_len, span, *refs),
        in_specs=[vmem] * 4,
        out_specs=vmem,
        out_shape=jax.ShapeDtypeStruct((n_pairs, share + span + n_src, tile), jnp.bfloat16),
        scratch_shapes=[
            pltpu.VMEM((slot, channels), jnp.float32),
            *[pltpu.VMEM((edge, channels), jnp.float32)] * 4,
            *[pltpu.VMEM((n_blocks, slot, tile), jnp.bfloat16)] * 2,
            pltpu.VMEM((seg_len, tile), jnp.bfloat16),
            *[pltpu.VMEM((n_tiles, 2, span), jnp.float32)] * 2,
            pltpu.VMEM((n_src, span), jnp.bfloat16),
            pltpu.VMEM((n_pairs, share + span + n_src, tile), jnp.bfloat16),
            pltpu.VMEM((144, 3 * depth), jnp.bfloat16),
            dma((2,)), dma((2,)),
            *[dma((n_blocks,))] * 4,
            *[dma((n_pairs,))] * 4,
        ],
        compiler_params=pltpu.CompilerParams(collective_id=0, has_side_effects=True),
        name="exchange",
    )(raw_strain[0], aa_row, taps, src_channels)

    groups = share // LAG_GROUP
    reach = n_pairs * (span + LAG_GROUP)
    whole = lambda *shape: pl.BlockSpec(shape, lambda i: (0,) * len(shape))
    xcorr = pl.pallas_call(
        lambda *refs: correlate_kernel(span, n_src, *refs),
        grid=(LAG_GROUP // STEP_LAGS,),
        in_specs=[whole(*got.shape), whole(n_src, 1), whole(n_src, 1)],
        out_specs=pl.BlockSpec((groups, STEP_LAGS, n_src, tile), lambda i: (0, i, 0, 0)),
        out_shape=jax.ShapeDtypeStruct((groups, LAG_GROUP, n_src, tile), jnp.float32),
        scratch_shapes=[
            pltpu.VMEM((STEP_LAGS * n_src, reach), jnp.bfloat16),
            pltpu.VMEM((reach, groups * tile), jnp.bfloat16),
            pltpu.VMEM((n_src, reach), jnp.float32),
        ],
        name="correlate",
    )(got, recv_lo.reshape(n_src, 1), recv_hi.reshape(n_src, 1))
    return xcorr.reshape(1, share, n_src, tile)


def solution(mesh):
    placed = (P("pair", "blk", None), P(), P(), P(), P("blk", None), P("blk", None))
    return jax.shard_map(
        body, mesh=mesh, in_specs=placed, out_specs=P("blk", "pair", None, None), check_vma=False
    )
```

time: 83.4 us -> 55.8 us (0.67)
  Pallas kernels: 10.4 us -> 50.4 us
  starting transfers between devices: 30.9 us -> 0 us
  waiting for transfers between devices: 29.4 us -> 0 us
  other arithmetic: 5.73 us -> 2.48 us
  local copies, waits for them, and re-layouts: 5.69 us -> 2.69 us
    pallas_call x1, Pallas kernels: 2.25 us -> 42.2 us  [body(): pl.pallas_call(lambda *refs: exchange_kernel(n_blocks, n_pairs, short_len...]
    all_to_all x3 -> x0, waiting for transfers between devices: 27.8 us -> none  [the longest x1 12.4 us: body(): lax.all_to_all(decimated, 'blk', split_axis=1, concat_axis=0, tiled=True)]
    all_to_all x3 -> x0, starting transfers between devices: 23.8 us -> none  [the longest x1 13.6 us: body(): lax.all_to_all(decimated, 'blk', split_axis=1, concat_axis=0, tiled=True)]
    ppermute x2 -> x0, starting transfers between devices: 7.07 us -> none  [the longest x1 5.15 us: body(): lax.ppermute(partial[:before], 'blk', [(i + 1, i) for i in range(ends)])]
    concatenate x4 -> x0, other arithmetic: 2.87 us -> none  [the longest x1 1.8 us: body(): jnp.concatenate([windows, jnp.broadcast_to(sources[None], (n_pairs, n_src...]
    broadcast_in_dim x1 -> x2, other arithmetic: 0.01 us -> 2.48 us  [the longest x1 1.25 us: body(): jnp.pad(white_taps.astype(jnp.float32), (0, 4 * BLOCK - white_taps.shape[...]
    ppermute x2 -> x0, waiting for transfers between devices: 1.61 us -> none  [the longest x1 1.42 us: body(): lax.ppermute(partial[before + short_len:], 'blk', [(i, i + 1) for i in ra...]
    pallas_call x1 -> x0, local copies, waits for them, and re-layouts: 1.41 us -> none  [body(): pl.pallas_call(lambda *refs: whiten_kernel(span, n_pairs, *refs), out_sha...]
  transfers between devices with their start and end apart: 5 -> 0, of which waited for: 5 -> 0; matrix products, arithmetic and copies ran while one was open for 5% -> 0% of each run, Pallas kernels for 0% -> 0%
where the time goes in v2:
time: 55.8 us; the launch traced here: 55.6 us
  Pallas kernels  50.4 us (90%)
  local copies, waits for them, and re-layouts  2.69 us (5%)
  other arithmetic  2.48 us (4%)
    pallas_call x1, Pallas kernels, body(): pl.pallas_call(lambda *refs: exchange_kernel(n_blocks, n_pairs, short_len...  42.2 us
    pallas_call x1, Pallas kernels, body(): pl.pallas_call(lambda *refs: correlate_kernel(span, n_src, *refs), grid=(...  8.18 us
    reshape x1, local copies, waits for them, and re-layouts, body(): recv_lo.reshape(n_src, 1)  1.34 us
    reshape x1, local copies, waits for them, and re-layouts, body(): recv_hi.reshape(n_src, 1)  1.34 us
    broadcast_in_dim x1, other arithmetic, body(): jnp.pad(white_taps.astype(jnp.float32), (0, 4 * BLOCK - white_taps.shape[...  1.25 us
    broadcast_in_dim x1, other arithmetic, body(): aa_row = jnp.pad(aa_taps.astype(jnp.float32), (0, aa_width - KA))[None]  1.23 us

profile of v2, /device:TPU:1, one launch (start us, length us, event | category | flops | bytes accessed | tf_op | source)
XLA Modules:
  0.0 55.6 jit_solution(17113976769164916895)
XLA Ops:
  0.0 1.2 %pad_convert_fusion.1 = f32[512]{0:T(512)} fusion(bf16[64]{0:T(256)(128)(2,1)} %param.7), kind=kLoop, calls=%fused_computation.1 | loop fusion | flops 512 | bytes 2176 | tf_op jit(solution)/shard_map/broadcast_in_dim | solution.py:277
  1.2 1.2 %pad_convert_fusion = f32[512]{0:T(512)} fusion(bf16[255]{0:T(256)(128)(2,1)} %param.8), kind=kLoop, calls=%fused_computation | loop fusion | flops 512 | bytes 2558 | tf_op jit(solution)/shard_map/broadcast_in_dim | solution.py:278
  2.5 1.3 %copy.7.refs_1_ = s32[64,1]{1,0:T(8,128)} copy(s32[64,1]{0,1:T(1,128)} %bitcast.9) | data formatting | bytes 512 | tf_op jit(solution)/shard_map/reshape | solution.py:319
  3.8 1.3 %copy.8.refs_2_ = s32[64,1]{1,0:T(8,128)} copy(s32[64,1]{0,1:T(1,128)} %bitcast.10) | data formatting | bytes 512 | tf_op jit(solution)/shard_map/reshape | solution.py:319
  5.2 42.2 %exchange.1.refs_0_ = bf16[4,448,128]{2,1,0:T(8,128)(2,1)} custom-call(bf16[144,8192]{1,0:T(8,128)(2,1)} %bitcast.6, f32[1,512]{1,0:T(1,128)} %bitcast.7, f32[1,512]{1,0:T(1,128)} %bitcast.8, s32[64,64]{1,0:T(8,128)} %refs_3_.1), custom_call_target="tpu_custom_call" | custom-call | tf_op jit(solution)/shard_map/exchange/pallas_call | solution.py:282
  47.4 8.2 %correlate.1 = f32[4,64,64,128]{3,2,1,0:T(8,128)} custom-call(bf16[4,448,128]{2,1,0:T(8,128)(2,1)} %exchange.1.refs_0_, s32[64,1]{1,0:T(8,128)} %copy.7.refs_1_, s32[64,1]{1,0:T(8,128)} %copy.8.refs_2_), custom_call_target="tpu_custom_call" | custom-call | tf_op jit(solution)/shard_map/correlate/pallas_call | solution.py:307

commit v3 on v2

--- a/solution.py
+++ b/solution.py
@@ -23,13 +23,23 @@
     return -(-value // unit) * unit
 
 
+def turned(row):
+    square = (row.shape[1], row.shape[1])
+    diagonal = lax.broadcasted_iota(jnp.int32, square, 0) == lax.broadcasted_iota(
+        jnp.int32, square, 1
+    )
+    across = jnp.broadcast_to(row, square).astype(jnp.float32)
+    return jnp.sum(jnp.where(diagonal, across, 0.0), axis=1, keepdims=True).astype(jnp.int32)
+
+
 def exchange_kernel(
     n_blk, n_pair, rows, span,
-    raw_ref, aa_ref, taps_ref, src_ref, out_ref,
+    raw_hbm, aa_in, taps_in, src_ref, out_ref,
+    raw_ref, aa_ref, taps_ref,
     own_ref, to_prev, to_next, from_prev, from_next, dec_ref, recv_ref,
     white_ref, offer_ref, taken_ref, pick_ref, got_ref, expand_ref,
     edge_send, edge_recv, dec_send, dec_recv, src_send, src_recv,
-    win_send, win_recv, pick_send, pick_recv,
+    win_send, win_recv, pick_send, pick_recv, raw_sem,
 ):
     me = lax.axis_index("blk")
     seg = lax.axis_index("pair")
@@ -52,6 +62,17 @@
     for step in range(1, n_pair):
         pl.semaphore_signal(barrier, inc=1, device_id={"pair": lax.rem(seg + step, n_pair)})
 
+    chunk = 8 * tile
+
+    def raw_copy(index):
+        cols = pl.ds(pl.multiple_of(index * chunk, chunk), chunk)
+        return pltpu.make_async_copy(raw_hbm.at[:, cols], raw_ref.at[:, cols], raw_sem.at[index])
+
+    for index in range(n_blk // 8):
+        raw_copy(index).start()
+    for wide_ref, given in ((aa_ref, aa_in), (taps_ref, taps_in)):
+        wide_ref[...] = jnp.zeros(wide_ref.shape, wide_ref.dtype)
+        wide_ref[:, : given.shape[0]] = given[...].astype(jnp.float32).reshape(1, given.shape[0])
     width = aa_ref.shape[1]
     lead = 2 * edge
     octets = []
@@ -60,9 +81,9 @@
         shifted = pltpu.roll(jnp.broadcast_to(aa_ref[...], (8, width)), shift, 1)
         octets.append(pltpu.roll(shifted, 0, 1, stride=DECIM, stride_axis=0))
     matrix = jnp.concatenate(octets, axis=0)[:, :raw_len].astype(jnp.bfloat16)
-    chunk = 8 * tile
 
     def decimate(index, carry):
+        raw_copy(index).wait()
         cols = pl.ds(pl.multiple_of(index * chunk, chunk), chunk)
         product = dot(matrix, raw_ref[:, cols])
         own_ref[:, cols] = product[lead : lead + slot]
@@ -142,13 +163,7 @@
         jnp.where(lane == channel, 1.0, 0.0).astype(jnp.bfloat16) for channel in (first, last)
     ]
     row = src_ref[pl.ds(me, 1), :]
-    square = (n_src, n_src)
-    across = jnp.broadcast_to(row, square).astype(jnp.float32)
-    diagonal = lax.broadcasted_iota(jnp.int32, square, 0) == lax.broadcasted_iota(
-        jnp.int32, square, 1
-    )
-    column = jnp.sum(jnp.where(diagonal, across, 0.0), axis=1, keepdims=True)
-    column = column.astype(jnp.int32)
+    column = turned(row)
     same = (row // tile) == (column // tile)
     later = jnp.max(jnp.where(same & (row < column), 1.0, 0.0), axis=1, keepdims=True)
     owner = lax.broadcasted_iota(jnp.int32, (n_src, n_blk), 1) == (column // tile)
@@ -203,6 +218,7 @@
         )
 
     pair_peers = [lax.rem(seg + step, n_pair) for step in range(1, n_pair)]
+    pair_peers = pair_peers[1:] + pair_peers[:1]
     lax.fori_loop(1, n_blk, send_source, 0)
     for peer in pair_peers:
         window_copy(peer, seg).start()
@@ -223,7 +239,7 @@
     out_ref[...] = got_ref[...]
 
 
-def correlate_kernel(span, n_src, got_ref, low_ref, high_ref, out_ref, lhs_ref, rhs_ref, src_ref):
+def correlate_kernel(span, n_src, got_ref, low_ref, high_ref, out_ref, lhs_ref, rhs_ref, src_ref, mask_ref):
     step = pl.program_id(0)
     segments, _, tile = got_ref.shape
     groups = out_ref.shape[0]
@@ -241,21 +257,23 @@
                     seg, group * LAG_GROUP : group * LAG_GROUP + reach, :
                 ]
         src_ref[...] = jnp.concatenate(pieces, axis=1)
+        low, high = turned(low_ref[...]), turned(high_ref[...])
+        position = lax.broadcasted_iota(jnp.int32, (n_src, tile), 1)
+        inside = (position >= low) & (position < high)
+        scale = 1.0 / math.sqrt(span * segments)
+        mask_ref[...] = jnp.where(inside, jnp.float32(scale), jnp.float32(0.0))
 
     base = src_ref[...]
     for lag in range(STEP_LAGS):
         rolled = pltpu.roll(base, lag, 1) if lag else base
         lhs_ref[lag * n_src : (lag + 1) * n_src, :] = rolled.astype(jnp.bfloat16)
     src_ref[...] = pltpu.roll(base, STEP_LAGS, 1)
-    scale = 1.0 / math.sqrt(span * segments)
-    position = lax.broadcasted_iota(jnp.int32, (n_src, tile), 1)
-    inside = (position >= low_ref[...]) & (position < high_ref[...])
-    mask = jnp.where(inside, jnp.float32(scale), jnp.float32(0.0))
+    mask = mask_ref[...]
     for group in range(0, groups, 2):
         product = dot(lhs_ref[...], rhs_ref[:, group * tile : (group + 2) * tile])
         for half in range(2):
             piece = product[:, half * tile : (half + 1) * tile].reshape(STEP_LAGS, n_src, tile)
-            out_ref[group + half] = jnp.where(inside[None], piece * mask[None], 0.0)
+            out_ref[group + half] = piece * mask[None]
 
 
 def body(raw_strain, aa_taps, white_taps, src_channels, recv_lo, recv_hi):
@@ -274,17 +292,18 @@
     slot = rounded(short_len, 16)
     edge = KA // 2 // DECIM
     aa_width = rounded(DECIM * (slot + 3 * edge) + KA + KA // 2, BLOCK)
-    aa_row = jnp.pad(aa_taps.astype(jnp.float32), (0, aa_width - KA))[None]
-    taps = jnp.pad(white_taps.astype(jnp.float32), (0, 4 * BLOCK - white_taps.shape[0]))[None]
     depth = 144 // short_len * slot
     dma = pltpu.SemaphoreType.DMA
     vmem = pl.BlockSpec(memory_space=pltpu.VMEM)
     got = pl.pallas_call(
         lambda *refs: exchange_kernel(n_blocks, n_pairs, short_len, span, *refs),
-        in_specs=[vmem] * 4,
+        in_specs=[pl.BlockSpec(memory_space=pl.ANY)] + [vmem] * 3,
         out_specs=vmem,
         out_shape=jax.ShapeDtypeStruct((n_pairs, share + span + n_src, tile), jnp.bfloat16),
         scratch_shapes=[
+            pltpu.VMEM((raw_len, channels), raw_strain.dtype),
+            pltpu.VMEM((1, aa_width), jnp.float32),
+            pltpu.VMEM((1, 4 * BLOCK), jnp.float32),
             pltpu.VMEM((slot, channels), jnp.float32),
             *[pltpu.VMEM((edge, channels), jnp.float32)] * 4,
             *[pltpu.VMEM((n_blocks, slot, tile), jnp.bfloat16)] * 2,
@@ -296,10 +315,11 @@
             dma((2,)), dma((2,)),
             *[dma((n_blocks,))] * 4,
             *[dma((n_pairs,))] * 4,
+            dma((n_blocks // 8,)),
         ],
         compiler_params=pltpu.CompilerParams(collective_id=0, has_side_effects=True),
         name="exchange",
-    )(raw_strain[0], aa_row, taps, src_channels)
+    )(raw_strain[0], aa_taps, white_taps, src_channels)
 
     groups = share // LAG_GROUP
     reach = n_pairs * (span + LAG_GROUP)
@@ -307,16 +327,17 @@
     xcorr = pl.pallas_call(
         lambda *refs: correlate_kernel(span, n_src, *refs),
         grid=(LAG_GROUP // STEP_LAGS,),
-        in_specs=[whole(*got.shape), whole(n_src, 1), whole(n_src, 1)],
+        in_specs=[whole(*got.shape), whole(1, n_src), whole(1, n_src)],
         out_specs=pl.BlockSpec((groups, STEP_LAGS, n_src, tile), lambda i: (0, i, 0, 0)),
         out_shape=jax.ShapeDtypeStruct((groups, LAG_GROUP, n_src, tile), jnp.float32),
         scratch_shapes=[
             pltpu.VMEM((STEP_LAGS * n_src, reach), jnp.bfloat16),
             pltpu.VMEM((reach, groups * tile), jnp.bfloat16),
             pltpu.VMEM((n_src, reach), jnp.float32),
+            pltpu.VMEM((n_src, tile), jnp.float32),
         ],
         name="correlate",
-    )(got, recv_lo.reshape(n_src, 1), recv_hi.reshape(n_src, 1))
+    )(got, recv_lo, recv_hi)
     return xcorr.reshape(1, share, n_src, tile)
 
 

time: 55.8 us -> 49.7 us (0.89)
  local copies, waits for them, and re-layouts: 2.69 us -> 0 us
  other arithmetic: 2.48 us -> 0 us
  Pallas kernels: 50.4 us -> 49.5 us
    reshape x2 -> x0, local copies, waits for them, and re-layouts: 2.69 us -> none  [the longest x1 1.34 us: body(): recv_lo.reshape(n_src, 1)]
    broadcast_in_dim x2 -> x0, other arithmetic: 2.48 us -> none  [the longest x1 1.25 us: body(): jnp.pad(white_taps.astype(jnp.float32), (0, 4 * BLOCK - white_taps.shape[...]
    pallas_call x1, Pallas kernels: 42.2 us -> 41.3 us  [body(): pl.pallas_call(lambda *refs: exchange_kernel(n_blocks, n_pairs, short_len...]
where the time goes in v3:
time: 49.7 us; the launch traced here: 49.5 us
  Pallas kernels  49.5 us (100%)
    pallas_call x1, Pallas kernels, body(): pl.pallas_call(lambda *refs: exchange_kernel(n_blocks, n_pairs, short_len...  41.3 us
    pallas_call x1, Pallas kernels, body(): pl.pallas_call(lambda *refs: correlate_kernel(span, n_src, *refs), grid=(...  8.2 us

profile of v3, /device:TPU:1, one launch (start us, length us, event | category | flops | bytes accessed | tf_op | source)
XLA Modules:
  0.0 49.5 jit_solution(11568069826345820836)
XLA Ops:
  0.0 41.3 %exchange.1.refs_0_ = bf16[4,448,128]{2,1,0:T(8,128)(2,1)} custom-call(bf16[144,8192]{1,0:T(8,128)(2,1)} %bitcast.2, bf16[64]{0:T(256)(128)(2,1)} %refs_1_.2, bf16[255]{0:T(256)(128)(2,1)} %refs_2_.2, s32[64,64]{1,0:T(8,128)} %refs_3_.1), custom_call_target="tpu_custom_call" | custom-call | tf_op jit(solution)/shard_map/exchange/pallas_call | solution.py:298
  41.3 8.2 %correlate.1 = f32[4,64,64,128]{3,2,1,0:T(8,128)} custom-call(bf16[4,448,128]{2,1,0:T(8,128)(2,1)} %exchange.1.refs_0_, s32[1,64]{1,0:T(1,128)} %refs_1_.3, s32[1,64]{1,0:T(1,128)} %refs_2_.3), custom_call_target="tpu_custom_call" | custom-call | tf_op jit(solution)/shard_map/correlate/pallas_call | solution.py:327

commit v4 on v3

--- a/solution.py
+++ b/solution.py
@@ -36,7 +36,7 @@
     n_blk, n_pair, rows, span,
     raw_hbm, aa_in, taps_in, src_ref, out_ref,
     raw_ref, aa_ref, taps_ref,
-    own_ref, to_prev, to_next, from_prev, from_next, dec_ref, recv_ref,
+    edges_ref, to_prev, to_next, from_prev, from_next, dec_ref, recv_ref,
     white_ref, offer_ref, taken_ref, pick_ref, got_ref, expand_ref,
     edge_send, edge_recv, dec_send, dec_recv, src_send, src_recv,
     win_send, win_recv, pick_send, pick_recv, raw_sem,
@@ -50,6 +50,8 @@
     window = share + span
     n_src = pick_ref.shape[0]
     edge = KA // 2 // DECIM
+    inner = rows - 2 * edge
+    inner_slot = slot - 16
 
     recv_ref[...] = jnp.zeros(recv_ref.shape, recv_ref.dtype)
     barrier = pltpu.get_barrier_semaphore()
@@ -76,7 +78,7 @@
     width = aa_ref.shape[1]
     lead = 2 * edge
     octets = []
-    for start in range(0, rounded(lead + max(slot, rows + edge), 8), 8):
+    for start in range(0, rounded(lead + slot + edge, 8), 8):
         shift = (DECIM * (start - lead) - KA // 2) % width
         shifted = pltpu.roll(jnp.broadcast_to(aa_ref[...], (8, width)), shift, 1)
         octets.append(pltpu.roll(shifted, 0, 1, stride=DECIM, stride_axis=0))
@@ -86,7 +88,11 @@
         raw_copy(index).wait()
         cols = pl.ds(pl.multiple_of(index * chunk, chunk), chunk)
         product = dot(matrix, raw_ref[:, cols])
-        own_ref[:, cols] = product[lead : lead + slot]
+        edges_ref[0:edge, cols] = product[lead : lead + edge]
+        edges_ref[edge : 2 * edge, cols] = product[lead + rows - edge : lead + rows]
+        inside = product[lead + edge : lead + edge + inner_slot].astype(jnp.bfloat16)
+        for part in range(8):
+            dec_ref[index * 8 + part, 0:inner_slot] = inside[:, part * tile : (part + 1) * tile]
         to_prev[:, cols] = product[lead - edge : lead]
         to_next[:, cols] = product[lead + rows : lead + rows + edge]
         return carry
@@ -104,6 +110,51 @@
     )
     up.start()
     down.start()
+
+    def block_copy(peer, place, piece):
+        part = pl.ds(0, inner) if piece == 0 else pl.ds(inner_slot, 2 * edge)
+        return pltpu.make_async_remote_copy(
+            dec_ref.at[peer, part], recv_ref.at[place, part],
+            dec_send.at[piece, peer], dec_recv.at[piece, place], device_id={"blk": peer},
+        )
+
+    def send_block(piece):
+        def send(step, carry):
+            block_copy(lax.rem(me + step, n_blk), me, piece).start()
+            return carry
+
+        lax.fori_loop(1, n_blk, send, 0)
+
+    def wait_block(step, carry):
+        peer = lax.rem(me + step, n_blk)
+        for piece in range(2):
+            copy = block_copy(peer, peer, piece)
+            copy.wait_send()
+            copy.wait_recv()
+        return carry
+
+    send_block(0)
+    up.wait()
+    down.wait()
+
+    def finish(index, carry):
+        cols = pl.ds(pl.multiple_of(index * chunk, chunk), chunk)
+        head = edges_ref[0:edge, cols] + jnp.where(me > 0, from_prev[:, cols], 0.0)
+        foot = edges_ref[edge : 2 * edge, cols]
+        foot += jnp.where(me < n_blk - 1, from_next[:, cols], 0.0)
+        block = jnp.concatenate([head, foot], axis=0).astype(jnp.bfloat16)
+        for part in range(8):
+            dec_ref[index * 8 + part, inner_slot : inner_slot + 2 * edge] = block[
+                :, part * tile : (part + 1) * tile
+            ]
+        return carry
+
+    lax.fori_loop(0, n_blk // 8, finish, 0)
+    send_block(1)
+    recv_ref[me, 0:inner] = dec_ref[me, 0:inner]
+    recv_ref[me, inner_slot : inner_slot + 2 * edge] = dec_ref[
+        me, inner_slot : inner_slot + 2 * edge
+    ]
 
     period = 144 // rows
     depth = period * slot
@@ -113,45 +164,14 @@
     ).astype(jnp.bfloat16)
     wide = lax.broadcasted_iota(jnp.int32, (reach, 3 * depth), 1)
     tall = lax.broadcasted_iota(jnp.int32, (reach, 3 * depth), 0)
-    inner = lax.rem(wide, slot)
-    hit = (tall == (wide // slot) * rows + inner) & (inner < rows)
+    place = lax.rem(wide, slot)
+    head, foot = place - inner_slot, place - inner_slot - 2 * edge + rows
+    time = jnp.where(place < inner_slot, place + edge, jnp.where(head < edge, head, foot))
+    used = (place < inner) | ((head >= 0) & (head < 2 * edge))
+    hit = (tall == (wide // slot) * rows + time) & used
     expand_ref[...] = dot(compact, jnp.where(hit, 1.0, 0.0).astype(jnp.bfloat16)).astype(
         jnp.bfloat16
     )
-
-    up.wait()
-    down.wait()
-
-    def finish(index, carry):
-        cols = pl.ds(pl.multiple_of(index * chunk, chunk), chunk)
-        own_ref[0:edge, cols] += jnp.where(me > 0, from_prev[:, cols], 0.0)
-        own_ref[rows - edge : rows, cols] += jnp.where(me < n_blk - 1, from_next[:, cols], 0.0)
-        block = own_ref[:, cols].astype(jnp.bfloat16)
-        for part in range(8):
-            dec_ref[index * 8 + part] = block[:, part * tile : (part + 1) * tile]
-        return carry
-
-    lax.fori_loop(0, n_blk // 8, finish, 0)
-
-    def block_copy(peer, place):
-        return pltpu.make_async_remote_copy(
-            dec_ref.at[peer, pl.ds(0, rows)], recv_ref.at[place, pl.ds(0, rows)],
-            dec_send.at[peer], dec_recv.at[place], device_id={"blk": peer},
-        )
-
-    def send_block(step, carry):
-        block_copy(lax.rem(me + step, n_blk), me).start()
-        return carry
-
-    def wait_block(step, carry):
-        peer = lax.rem(me + step, n_blk)
-        copy = block_copy(peer, peer)
-        copy.wait_send()
-        copy.wait_recv()
-        return carry
-
-    lax.fori_loop(1, n_blk, send_block, 0)
-    recv_ref[me] = dec_ref[me]
 
     src = src_ref[...]
     belongs = (src // tile) == me
@@ -289,8 +309,8 @@
     n_tiles = src_channels.shape[0]
     share = LAGS // n_pairs
 
-    slot = rounded(short_len, 16)
     edge = KA // 2 // DECIM
+    slot = rounded(short_len - 2 * edge, 16) + 16
     aa_width = rounded(DECIM * (slot + 3 * edge) + KA + KA // 2, BLOCK)
     depth = 144 // short_len * slot
     dma = pltpu.SemaphoreType.DMA
@@ -304,7 +324,7 @@
             pltpu.VMEM((raw_len, channels), raw_strain.dtype),
             pltpu.VMEM((1, aa_width), jnp.float32),
             pltpu.VMEM((1, 4 * BLOCK), jnp.float32),
-            pltpu.VMEM((slot, channels), jnp.float32),
+            pltpu.VMEM((2 * edge, channels), jnp.float32),
             *[pltpu.VMEM((edge, channels), jnp.float32)] * 4,
             *[pltpu.VMEM((n_blocks, slot, tile), jnp.bfloat16)] * 2,
             pltpu.VMEM((seg_len, tile), jnp.bfloat16),
@@ -313,7 +333,8 @@
             pltpu.VMEM((n_pairs, share + span + n_src, tile), jnp.bfloat16),
             pltpu.VMEM((144, 3 * depth), jnp.bfloat16),
             dma((2,)), dma((2,)),
-            *[dma((n_blocks,))] * 4,
+            *[dma((2, n_blocks))] * 2,
+            *[dma((n_blocks,))] * 2,
             *[dma((n_pairs,))] * 4,
             dma((n_blocks // 8,)),
         ],

time: 49.7 us -> 49.5 us (level)
  no operation moved by 1% of the time
where the time goes in v4:
time: 49.5 us; the launch traced here: 49.3 us
  Pallas kernels  49.3 us (100%)
    pallas_call x1, Pallas kernels, body(): pl.pallas_call(lambda *refs: exchange_kernel(n_blocks, n_pairs, short_len...  41.1 us
    pallas_call x1, Pallas kernels, body(): pl.pallas_call(lambda *refs: correlate_kernel(span, n_src, *refs), grid=(...  8.21 us

profile of v4, /device:TPU:1, one launch (start us, length us, event | category | flops | bytes accessed | tf_op | source)
XLA Modules:
  0.0 49.3 jit_solution(17012972498382752553)
XLA Ops:
  0.0 41.1 %exchange.1.refs_0_ = bf16[4,448,128]{2,1,0:T(8,128)(2,1)} custom-call(bf16[144,8192]{1,0:T(8,128)(2,1)} %bitcast.2, bf16[64]{0:T(256)(128)(2,1)} %refs_1_.2, bf16[255]{0:T(256)(128)(2,1)} %refs_2_.2, s32[64,64]{1,0:T(8,128)} %refs_3_.1), custom_call_target="tpu_custom_call" | custom-call | tf_op jit(solution)/shard_map/exchange/pallas_call | solution.py:318
  41.1 8.2 %correlate.1 = f32[4,64,64,128]{3,2,1,0:T(8,128)} custom-call(bf16[4,448,128]{2,1,0:T(8,128)(2,1)} %exchange.1.refs_0_, s32[1,64]{1,0:T(1,128)} %refs_1_.3, s32[1,64]{1,0:T(1,128)} %refs_2_.3), custom_call_target="tpu_custom_call" | custom-call | tf_op jit(solution)/shard_map/correlate/pallas_call | solution.py:348
